TPU v7x, 32 devices: a whole 2x2x4 slice. The times are simulated.
32 devices in a mesh: dp: 8 (over y, x, core), tensor: 4 (over z).
Axes of the slice: x: 2, y: 2, z: 4, core: 2. Of those that a mesh axis runs over, the one named last changes fastest.
Arguments:
- inputs: bfloat16 [2048, 2048], P(('dp', 'tensor')), parts along dimension 0, may hold values from -6 to 6
- grad_out: bfloat16 [2048, 2048], P(('dp', 'tensor')), parts along dimension 0, may hold values from -6 to 6
- gate_weight: bfloat16 [2048, 7168], P(None, 'tensor'), may hold values from -6 to 6
- up_weight: bfloat16 [2048, 7168], P(None, 'tensor'), may hold values from -6 to 6
- down_weight: bfloat16 [7168, 2048], P('tensor'), may hold values from -6 to 6
Outputs:
- grad_inputs: bfloat16 [2048, 2048], P(('dp', 'tensor')), parts along dimension 0
- grad_gate: bfloat16 [16384, 7168], P('dp', 'tensor'), parts along dimension 0
- grad_up: bfloat16 [16384, 7168], P('dp', 'tensor'), parts along dimension 0
- grad_down: bfloat16 [57344, 2048], P(('dp', 'tensor')), parts along dimension 0
There are 8 independent parts, one for each index of `dp`. A program takes and returns all parts, laid end to end along the dimension named above; an argument that names none is the same for every part. Nothing has to cross between parts.
All inputs are finite; a program needn't handle non-finite values.
Results may differ from a plain program's by a relative error of at most 0.0049.
Values may be sent and summed in bfloat16 or wider, within the bound.
A program may use at most 128 MiB of HBM per device.

v0:
```python
import jax
import jax.numpy as jnp
from jax import lax
from jax.sharding import PartitionSpec as P

D = 2048
FF = 7168


def contract_last(left, right):
    return lax.dot_general(
        left, right, (((1,), (1,)), ((), ())), preferred_element_type=jnp.float32
    )


def contract_first(left, right):
    return lax.dot_general(
        left, right, (((0,), (0,)), ((), ())), preferred_element_type=jnp.float32
    )


def on_device(inputs, grad_out, gate_weight, up_weight, down_weight):
    tokens_all = lax.all_gather(inputs, "tensor", axis=0, tiled=True)
    grads_all = lax.all_gather(grad_out, "tensor", axis=0, tiled=True)
    inv_width = D ** (-0.5)
    inv_rows = tokens_all.shape[0] ** (-0.5)
    inv_hidden = (2 * FF) ** (-0.5)
    gate = jnp.dot(tokens_all, gate_weight, preferred_element_type=jnp.float32) * inv_width
    up = jnp.dot(tokens_all, up_weight, preferred_element_type=jnp.float32) * inv_width
    sig = jax.nn.sigmoid(gate)
    act = gate * sig
    hidden = (act * up).astype(jnp.bfloat16)
    d_hidden = contract_last(grads_all, down_weight) * inv_width
    grad_down = (contract_first(hidden, grads_all) * inv_rows).astype(jnp.bfloat16)
    d_gate = (d_hidden * up * sig * (1.0 + gate * (1.0 - sig))).astype(jnp.bfloat16)
    d_up = (d_hidden * act).astype(jnp.bfloat16)
    grad_gate = (contract_first(tokens_all, d_gate) * inv_rows).astype(jnp.bfloat16)
    grad_up = (contract_first(tokens_all, d_up) * inv_rows).astype(jnp.bfloat16)
    summed = lax.psum_scatter(
        contract_last(d_gate, gate_weight) * inv_hidden
        + contract_last(d_up, up_weight) * inv_hidden,
        "tensor",
        scatter_dimension=0,
        tiled=True,
    )
    grad_inputs = summed.astype(jnp.bfloat16)
    return (grad_inputs, grad_gate, grad_up, grad_down)


def solution(mesh):
    placed = (
        P(("dp", "tensor"), None),
        P(("dp", "tensor"), None),
        P(None, "tensor"),
        P(None, "tensor"),
        P("tensor", None),
    )
    return jax.shard_map(
        on_device,
        mesh=mesh,
        in_specs=placed,
        out_specs=(
            P(("dp", "tensor"), None),
            P("dp", "tensor"),
            P("dp", "tensor"),
            P(("dp", "tensor"), None),
        ),
        check_vma=False,
    )
```

profile of v0, /device:TPU:0, one launch (start us, length us, event | category | flops | bytes accessed | tf_op | source)
XLA Modules:
  0.0 139.9 jit_solution(8619819542554499196)
XLA Ops:
  7.2 0.0 all-gather.5.cloned.1.call-start
  7.2 0.7 all-gather.5.cloned.1.call-update
  7.9 0.0 all-gather.3.cloned.1.call-start
  7.9 0.7 all-gather.3.cloned.1.call-update
  8.6 0.0 reduce-scatter.2.cloned.1.call-start
  8.7 31.5 %all-gather.5.cloned.1.call-done = bf16[256,2048]{1,0:T(8,128)(2,1)} async-done(((bf16[64,2048]{1,0:T(8,128)(2,1)}), bf16[256,2048]{1,0:T(8,128)(2,1)}) %all-gather.5.cloned.1.call-update) | async-done | bytes 1048592 | tf_op jit(solution)/shard_map/all_gather | solution.py:23
  40.2 0.0 copy-start
  40.2 6.8 %convolution_multiply_fusion = f32[256,1792]{1,0:T(8,128)} fusion(bf16[256,2048]{1,0:T(8,128)(2,1)} %all-gather.5.cloned.1.call-done, bf16[2048,1792]{1,0:T(8,128)(2,1)} %param.7), kind=kOutput, calls=%fused_computation.5 | convolution fusion | flops 1879506944 | bytes 10223616 | tf_op jit(solution)/shard_map/dot_general | solution.py:28
  47.0 0.0 copy-done
  47.0 6.6 %convolution_multiply_fusion.1 = f32[256,1792]{1,0:T(8,128)} fusion(bf16[256,2048]{1,0:T(8,128)(2,1)S(1)} %copy-done, bf16[2048,1792]{1,0:T(8,128)(2,1)} %param.8), kind=kOutput, calls=%fused_computation.6 | convolution fusion | flops 1879506944 | bytes 10223616 | tf_op jit(solution)/shard_map/dot_general | solution.py:29
  53.6 15.6 %all-gather.3.cloned.1.call-done = bf16[256,2048]{1,0:T(8,128)(2,1)} async-done(((bf16[64,2048]{1,0:T(8,128)(2,1)}), bf16[256,2048]{1,0:T(8,128)(2,1)}) %all-gather.3.cloned.1.call-update) | async-done | bytes 1048592 | tf_op jit(solution)/shard_map/all_gather | solution.py:24
  69.3 7.1 %multiply_convert_fusion.4 = (bf16[256,1792]{1,0:T(8,128)(2,1)S(1)}, bf16[256,1792]{1,0:T(8,128)(2,1)S(1)}) fusion(f32[256,1792]{1,0:T(8,128)} %convolution_multiply_fusion, f32[256,1792]{1,0:T(8,128)} %convolution_multiply_fusion.1, bf16[256,2048]{1,0:T(8,128)(2,1)} %all-gather.3.cloned.1.call-done, bf16[1792,2048]{1,0:T(8,128)(2,1)} %param.9), kind=kOutput, calls=%fused_computation.11 | convolution fusion | flops 1885470720 | bytes 13893632 | tf_op jit(solution)/shard_map/dot_general | solution.py:11
  76.3 5.2 %fusion.6 = f32[256,2048]{1,0:T(8,128)S(1)} fusion(bf16[256,1792]{1,0:T(8,128)(2,1)S(1)} %get-tuple-element.9, bf16[2048,1792]{1,0:T(8,128)(2,1)} %param.7), kind=kOutput, calls=%fused_computation.16 | convolution fusion | flops 1879048192 | bytes 10354688 | tf_op jit(solution)/shard_map/dot_general | solution.py:11
  81.5 6.6 %fusion.2 = f32[256,2048]{1,0:T(8,128)} fusion(f32[256,2048]{1,0:T(8,128)S(1)} %fusion.6, bf16[256,1792]{1,0:T(8,128)(2,1)S(1)} %get-tuple-element.8, bf16[2048,1792]{1,0:T(8,128)(2,1)} %param.8), kind=kOutput, calls=%fused_computation.9 | convolution fusion | flops 1880096768 | bytes 12451840 | tf_op jit(solution)/shard_map/dot_general | solution.py:11
  88.1 0.0 reduce-scatter.2.cloned.1.call-update
  88.1 5.2 %fusion.1 = bf16[2048,1792]{0,1:T(8,128)(2,1)} fusion(bf16[256,1792]{1,0:T(8,128)(2,1)S(1)} %get-tuple-element.8, bf16[256,2048]{1,0:T(8,128)(2,1)S(1)} %copy-done), kind=kOutput, calls=%fused_computation.4 | convolution fusion | flops 1886388224 | bytes 9306112 | tf_op jit(solution)/shard_map/dot_general | solution.py:17
  93.2 10.1 %copy.10 = bf16[2048,1792]{1,0:T(8,128)(2,1)} copy(bf16[2048,1792]{0,1:T(8,128)(2,1)} %fusion.1) | data formatting | bytes 14680064
  103.3 5.1 %fusion = bf16[2048,1792]{0,1:T(8,128)(2,1)} fusion(bf16[256,1792]{1,0:T(8,128)(2,1)S(1)} %get-tuple-element.9, bf16[256,2048]{1,0:T(8,128)(2,1)S(1)} %copy-done), kind=kOutput, calls=%fused_computation.3 | convolution fusion | flops 1886388224 | bytes 9306112 | tf_op jit(solution)/shard_map/dot_general | solution.py:17
  108.5 0.0 copy-start.1
  108.5 0.0 copy-start.2
  108.5 10.1 %copy.9 = bf16[2048,1792]{1,0:T(8,128)(2,1)} copy(bf16[2048,1792]{0,1:T(8,128)(2,1)} %fusion) | data formatting | bytes 14680064
  118.6 0.0 copy-done.1
  118.6 0.0 copy-done.2
  118.6 6.8 %multiply_convert_fusion = bf16[1792,2048]{1,0:T(8,128)(2,1)} fusion(bf16[256,2048]{1,0:T(8,128)(2,1)S(1)} %copy-done.1, f32[256,1792]{1,0:T(8,128)} %convolution_multiply_fusion.1, f32[256,1792]{1,0:T(8,128)S(1)} %copy-done.2), kind=kOutput, calls=%fused_computation | convolution fusion | flops 1889140736 | bytes 12058624 | tf_op jit(solution)/shard_map/dot_general | solution.py:17
  125.4 6.2 %reduce-scatter.2.cloned.1.call-done = f32[64,2048]{1,0:T(8,128)} async-done(((f32[256,2048]{1,0:T(8,128)}), f32[64,2048]{1,0:T(8,128)}) %reduce-scatter.2.cloned.1.call-update) | async-done | bytes 524304 | tf_op jit(solution)/shard_map/reduce_scatter | solution.py:39
  131.6 1.8 %convert_element_type.29 = bf16[64,2048]{1,0:T(8,128)(2,1)} convert(f32[64,2048]{1,0:T(8,128)} %reduce-scatter.2.cloned.1.call-done) | non-fusion elementwise | flops 131072 | bytes 786432 | tf_op jit(solution)/shard_map/convert_element_type | solution.py:46
Async XLA Ops:
  7.2 33.1 %all-gather.5.cloned.1.call-start = ((), (), s32[]{:S(2)}) async-start(), calls=%async_computation.2 | async-start | bytes 1310720 | tf_op jit(solution)/shard_map/all_gather | solution.py:23
  7.9 61.4 %all-gather.3.cloned.1.call-start = ((), (), s32[]{:S(2)}) async-start(), calls=%async_computation.1 | async-start | bytes 1310720 | tf_op jit(solution)/shard_map/all_gather | solution.py:24
  8.6 122.9 %reduce-scatter.2.cloned.1.call-start = ((), (), s32[]{:S(2)}) async-start(), calls=%async_computation.3 | async-start | bytes 2621440 | tf_op jit(solution)/shard_map/reduce_scatter | solution.py:39
  40.2 6.8 %copy-start = (bf16[256,2048]{1,0:T(8,128)(2,1)S(1)}, bf16[256,2048]{1,0:T(8,128)(2,1)}, u32[]{:S(2)}) copy-start(bf16[256,2048]{1,0:T(8,128)(2,1)} %all-gather.5.cloned.1.call-done) | copy-start | bytes 3145732
  108.5 10.1 %copy-start.1 = (bf16[256,2048]{1,0:T(8,128)(2,1)S(1)}, bf16[256,2048]{1,0:T(8,128)(2,1)}, u32[]{:S(2)}) copy-start(bf16[256,2048]{1,0:T(8,128)(2,1)} %all-gather.3.cloned.1.call-done) | copy-start | bytes 3145732
  108.5 10.1 %copy-start.2 = (f32[256,1792]{1,0:T(8,128)S(1)}, f32[256,1792]{1,0:T(8,128)}, u32[]{:S(2)}) copy-start(f32[256,1792]{1,0:T(8,128)} %convolution_multiply_fusion) | copy-start | bytes 5505028
Sparse Core Ops, SparseCore 0:
  9.6 30.6 all-gather.4
  41.8 27.4 all-gather.2
  88.2 43.3 reduce-scatter.1
where the time goes:
time: 141 us; the launch traced here: 140 us
  waiting for transfers between devices  54.7 us (39%)
  matrix products  49.3 us (35%)
  local copies, waits for them, and re-layouts  20.2 us (14%)
  between operations  13.8 us (10%)
  other arithmetic  1.77 us (1%)
    all_gather x1, waiting for transfers between devices, on_device(): tokens_all = lax.all_gather(inputs, 'tensor', axis=0, tiled=True)  31.5 us
    unnamed x8, local copies, waits for them, and re-layouts  20.2 us
    dot_general x3, matrix products, contract_last(): lax.dot_general(left, right, (((1,), (1,)), ((), ())), preferred_element_...  18.8 us
    dot_general x3, matrix products, contract_first(): lax.dot_general(left, right, (((0,), (0,)), ((), ())), preferred_element_...  17.1 us
    all_gather x1, waiting for transfers between devices, on_device(): grads_all = lax.all_gather(grad_out, 'tensor', axis=0, tiled=True)  15.6 us
    dot_general x1, matrix products, on_device(): jnp.dot(tokens_all, gate_weight, preferred_element_type=jnp.float32)  6.77 us
    dot_general x1, matrix products, on_device(): jnp.dot(tokens_all, up_weight, preferred_element_type=jnp.float32)  6.64 us
    reduce_scatter x1, waiting for transfers between devices, on_device(): lax.psum_scatter(contract_last(d_gate, gate_weight) * inv_hidden + contra...  6.19 us
  transfers between devices with their start and end apart: 3, of which 3 were waited for; matrix products, arithmetic and copies ran while one was open for 36% of the time, Pallas kernels for 0%

commit v1 on v0

--- a/solution.py
+++ b/solution.py
@@ -1,3 +1,4 @@
+import functools
 import jax
 import jax.numpy as jnp
 from jax import lax
@@ -5,6 +6,32 @@
 
 D = 2048
 FF = 7168
+
+
+def report_the_task(panel, where_dim):
+    fan = jax.lax.psum(1, axis_name="tensor")
+    nodes = list(map(lambda w: (w, (w + 1) % fan), range(fan)))
+    r1 = range(fan)
+    view_out = map(lambda w: (w, (w - 1) % fan), r1)
+    pile = list(view_out)
+    earlier, block_next = ([panel], [panel])
+    for _ in range(fan // 2):
+        earlier.append(jax.lax.ppermute(earlier[-1], axis_name="tensor", perm=nodes))
+    jj = 0
+    while jj < (fan - 1) // 2:
+        k_now = jax.lax.ppermute(block_next[-1], axis_name="tensor", perm=pile)
+        block_next.append(k_now)
+        jj += 1
+    a_now = jnp.concatenate([*earlier[::-1], *block_next[1:]], axis=where_dim)
+    passed = jnp.roll(
+        a_now,
+        shift=(jax.lax.axis_index("tensor") - fan // 2) * panel.shape[where_dim],
+        axis=where_dim,
+    )
+    return passed
+
+
+put_sector = functools.partial(report_the_task, where_dim=0)
 
 
 def contract_last(left, right):
@@ -20,7 +47,7 @@
 
 
 def on_device(inputs, grad_out, gate_weight, up_weight, down_weight):
-    tokens_all = lax.all_gather(inputs, "tensor", axis=0, tiled=True)
+    tokens_all = put_sector(inputs)
     grads_all = lax.all_gather(grad_out, "tensor", axis=0, tiled=True)
     inv_width = D ** (-0.5)
     inv_rows = tokens_all.shape[0] ** (-0.5)

time: 141 us -> 121 us (0.86)
  local copies, waits for them, and re-layouts: 20.2 us -> 1.15 us
  starting transfers between devices: 0.11 us -> 6.98 us
  waiting for transfers between devices: 54.7 us -> 50.5 us
  matrix products: 49.3 us -> 46.5 us
    all_gather x1 -> x0, waiting for transfers between devices: 31.5 us -> none  [on_device(): tokens_all = lax.all_gather(inputs, 'tensor', axis=0, tiled=True)]
    ppermute x0 -> x3, waiting for transfers between devices: none -> 21.4 us  [the longest x2 15.7 us: report_the_task(): jax.lax.ppermute(earlier[-1], axis_name='tensor', perm=nodes)]
    reduce_scatter x1, waiting for transfers between devices: 6.19 us -> 26.4 us  [on_device(): lax.psum_scatter(contract_last(d_gate, gate_weight) * inv_hidden + contra...]
    unnamed x8 -> x25, local copies, waits for them, and re-layouts: 20.2 us -> 1.13 us
    all_gather x1, waiting for transfers between devices: 15.6 us -> 2.71 us  [on_device(): grads_all = lax.all_gather(grad_out, 'tensor', axis=0, tiled=True)]
    ppermute x0 -> x3, starting transfers between devices: none -> 6.9 us  [the longest x1 3.82 us: report_the_task(): k_now = jax.lax.ppermute(block_next[-1], axis_name='tensor', perm=pile)]
    dot_general x1, matrix products: 6.64 us -> 3.33 us  [on_device(): jnp.dot(tokens_all, up_weight, preferred_element_type=jnp.float32)]
  transfers between devices with their start and end apart: 3 -> 5, of which waited for: 3 -> 5; matrix products, arithmetic and copies ran while one was open for 36% -> 23% of each run, Pallas kernels for 0% -> 0%
where the time goes in v1:
time: 121 us
  waiting for transfers between devices  50.5 us (42%)
  matrix products  46.5 us (38%)
  between operations  14.2 us (12%)
  starting transfers between devices  6.98 us (6%)
  other arithmetic  1.77 us (1%)
    reduce_scatter x1, waiting for transfers between devices, on_device(): lax.psum_scatter(contract_last(d_gate, gate_weight) * inv_hidden + contra...  26.4 us
    dot_general x3, matrix products, contract_last(): lax.dot_general(left, right, (((1,), (1,)), ((), ())), preferred_element_...  19.4 us
    dot_general x3, matrix products, contract_first(): lax.dot_general(left, right, (((0,), (0,)), ((), ())), preferred_element_...  17.2 us
    ppermute x2, waiting for transfers between devices, report_the_task(): jax.lax.ppermute(earlier[-1], axis_name='tensor', perm=nodes)  15.7 us
    dot_general x1, matrix products, on_device(): jnp.dot(tokens_all, gate_weight, preferred_element_type=jnp.float32)  6.57 us
    ppermute x1, waiting for transfers between devices, report_the_task(): k_now = jax.lax.ppermute(block_next[-1], axis_name='tensor', perm=pile)  5.73 us
    ppermute x1, starting transfers between devices, report_the_task(): k_now = jax.lax.ppermute(block_next[-1], axis_name='tensor', perm=pile)  3.82 us
    dot_general x1, matrix products, on_device(): jnp.dot(tokens_all, up_weight, preferred_element_type=jnp.float32)  3.33 us
  transfers between devices with their start and end apart: 5, of which 5 were waited for; matrix products, arithmetic and copies ran while one was open for 23% of the time, Pallas kernels for 0%

profile of v1, /device:TPU:0, one launch (start us, length us, event | category | flops | bytes accessed | tf_op | source)
XLA Modules:
  0.0 121.1 jit_solution(60469939136901588)
XLA Ops:
  7.2 0.0 copy-start
  7.2 0.0 all-gather.2.cloned.1.call-start
  7.2 3.1 %collective-permute-start = (bf16[64,2048]{1,0:T(8,128)(2,1)}, bf16[64,2048]{1,0:T(8,128)(2,1)S(1)}, u32[]{:S(2)}, u32[]{:S(2)}) collective-permute-start(bf16[64,2048]{1,0:T(8,128)(2,1)} %param.5), channel_id=1, source_target_pairs={{0,1},{1,2},{2,3},{3,0},{4,5},{5,6},{6,7},{7,4},{8,9},{9,10},{10,1... | collective-permute-start | bytes 786440 | tf_op jit(solution)/shard_map/ppermute | solution.py:19
  10.3 8.5 %collective-permute-done = bf16[64,2048]{1,0:T(8,128)(2,1)S(1)} collective-permute-done((bf16[64,2048]{1,0:T(8,128)(2,1)}, bf16[64,2048]{1,0:T(8,128)(2,1)S(1)}, u32[]{:S(2)}, u32[]{:S(2)}) %collective-permute-start) | collective-permute-done | bytes 262176 | tf_op jit(solution)/shard_map/ppermute | solution.py:19
  18.8 0.0 collective-permute-start.1
  18.8 3.8 %collective-permute-start.2 = (bf16[64,2048]{1,0:T(8,128)(2,1)}, bf16[64,2048]{1,0:T(8,128)(2,1)S(1)}, u32[]{:S(2)}, u32[]{:S(2)}) collective-permute-start(bf16[64,2048]{1,0:T(8,128)(2,1)} %param.5), channel_id=1, source_target_pairs={{0,3},{1,0},{2,1},{3,2},{4,7},{5,4},{6,5},{7,6},{8,11},{9,8},{10,9... | collective-permute-start | bytes 786440 | tf_op jit(solution)/shard_map/ppermute | solution.py:22
  22.7 0.0 all-gather.2.cloned.1.call-update
  22.7 0.0 reduce-scatter.2.cloned.1.call-start
  22.8 7.1 %collective-permute-done.1 = bf16[64,2048]{1,0:T(8,128)(2,1)S(1)} collective-permute-done((bf16[64,2048]{1,0:T(8,128)(2,1)S(1)}, bf16[64,2048]{1,0:T(8,128)(2,1)S(1)}, u32[]{:S(2)}, u32[]{:S(2)}) %collective-permute-start.1) | collective-permute-done | bytes 262176 | tf_op jit(solution)/shard_map/ppermute | solution.py:19
  29.9 1.0 constant_dynamic-update-slice_fusion.5
  30.9 5.7 %collective-permute-done.2 = bf16[64,2048]{1,0:T(8,128)(2,1)S(1)} collective-permute-done((bf16[64,2048]{1,0:T(8,128)(2,1)}, bf16[64,2048]{1,0:T(8,128)(2,1)S(1)}, u32[]{:S(2)}, u32[]{:S(2)}) %collective-permute-start.2) | collective-permute-done | bytes 262176 | tf_op jit(solution)/shard_map/ppermute | solution.py:22
  36.7 0.0 copy-done
  36.8 0.0 slice-start
  36.8 0.0 slice-start.1
  36.8 6.6 %convolution_multiply_fusion = f32[256,1792]{1,0:T(8,128)} fusion(bf16[2048,1792]{1,0:T(8,128)(2,1)} %param.7, bf16[512,2048]{1,0:T(8,128)(2,1)S(1)} %constant_dynamic-update-slice_fusion, s32[]{:T(128)S(6)} %select_n.14), kind=kOutput, calls=%fused_computation.3 | convolution fusion | flops 1879506944 | bytes 10223620 | tf_op jit(solution)/shard_map/dot_general | solution.py:55
  43.4 0.0 slice-done
  43.4 0.0 slice-done.1
  43.4 3.3 %convolution_multiply_fusion.1 = f32[256,1792]{1,0:T(8,128)} fusion(bf16[2048,1792]{1,0:T(8,128)(2,1)S(1)} %bitcast.12, bf16[512,2048]{1,0:T(8,128)(2,1)S(1)} %constant_dynamic-update-slice_fusion, s32[]{:T(128)S(6)} %select_n.14), kind=kOutput, calls=%fused_computation.4 | convolution fusion | flops 1879506944 | bytes 10223620 | tf_op jit(solution)/shard_map/dot_general | solution.py:56
  46.7 2.7 %all-gather.2.cloned.1.call-done = bf16[256,2048]{1,0:T(8,128)(2,1)} async-done(((bf16[64,2048]{1,0:T(8,128)(2,1)}), bf16[256,2048]{1,0:T(8,128)(2,1)}) %all-gather.2.cloned.1.call-update) | async-done | bytes 1048592 | tf_op jit(solution)/shard_map/all_gather | solution.py:51
  49.4 7.1 %multiply_convert_fusion.4 = (bf16[256,1792]{1,0:T(8,128)(2,1)S(1)}, bf16[256,1792]{1,0:T(8,128)(2,1)S(1)}) fusion(f32[256,1792]{1,0:T(8,128)} %convolution_multiply_fusion, f32[256,1792]{1,0:T(8,128)} %convolution_multiply_fusion.1, bf16[256,2048]{1,0:T(8,128)(2,1)} %all-gather.2.cloned.1.call-done, bf16[1792,2048]{1,0:T(8,128)(2,1)} %param.9), kind=kOutput, calls=%fused_computation.9 | convolution fusion | flops 1885470720 | bytes 13893632 | tf_op jit(solution)/shard_map/dot_general | solution.py:38
  56.5 0.0 copy-start.3
  56.5 0.0 copy-start.2
  56.5 5.8 %fusion.12 = f32[256,2048]{1,0:T(8,128)S(1)} fusion(bf16[256,1792]{1,0:T(8,128)(2,1)S(1)} %get-tuple-element.5, bf16[2048,1792]{1,0:T(8,128)(2,1)} %param.7), kind=kOutput, calls=%fused_computation.30 | convolution fusion | flops 1879048192 | bytes 10354688 | tf_op jit(solution)/shard_map/dot_general | solution.py:38
  62.3 0.0 copy-done.3
  62.4 0.0 copy-done.2
  62.4 6.6 %fusion = f32[256,2048]{1,0:T(8,128)} fusion(f32[256,2048]{1,0:T(8,128)S(1)} %fusion.12, bf16[256,1792]{1,0:T(8,128)(2,1)S(1)} %get-tuple-element.4, bf16[2048,1792]{1,0:T(8,128)(2,1)} %param.8), kind=kOutput, calls=%fused_computation.7 | convolution fusion | flops 1880096768 | bytes 12451840 | tf_op jit(solution)/shard_map/dot_general | solution.py:38
  68.9 0.0 reduce-scatter.2.cloned.1.call-update
  68.9 0.0 copy-start.4
  69.0 6.4 %multiply_convert_fusion.1 = bf16[2048,1792]{1,0:T(8,128)(2,1)} fusion(bf16[256,1792]{1,0:T(8,128)(2,1)} %copy-done.2, bf16[512,2048]{1,0:T(8,128)(2,1)S(1)} %constant_dynamic-update-slice_fusion, s32[]{:T(128)S(6)} %select_n.14), kind=kOutput, calls=%fused_computation.1 | convolution fusion | flops 1886388224 | bytes 9306116 | tf_op jit(solution)/shard_map/dot_general | solution.py:44
  75.4 0.0 copy-done.4
  75.4 0.0 copy-start.1
  75.4 0.0 copy-start.5
  75.4 0.0 copy-start.6
  75.4 5.4 %multiply_convert_fusion.2 = bf16[2048,1792]{1,0:T(8,128)(2,1)} fusion(bf16[256,1792]{1,0:T(8,128)(2,1)S(1)} %copy-done.4, bf16[512,2048]{1,0:T(8,128)(2,1)S(1)} %constant_dynamic-update-slice_fusion, s32[]{:T(128)S(6)} %select_n.14), kind=kOutput, calls=%fused_computation.2 | convolution fusion | flops 1886388224 | bytes 9306116 | tf_op jit(solution)/shard_map/dot_general | solution.py:44
  80.8 0.0 copy-done.1
  80.8 0.0 copy-done.5
  80.8 0.0 copy-done.6
  80.8 5.3 %multiply_convert_fusion = bf16[1792,2048]{1,0:T(8,128)(2,1)} fusion(bf16[256,2048]{1,0:T(8,128)(2,1)S(1)} %copy-done.1, f32[256,1792]{1,0:T(8,128)S(1)} %copy-done.6, f32[256,1792]{1,0:T(8,128)S(1)} %copy-done.5), kind=kOutput, calls=%fused_computation | convolution fusion | flops 1889140736 | bytes 12058624 | tf_op jit(solution)/shard_map/dot_general | solution.py:44
  86.2 26.4 %reduce-scatter.2.cloned.1.call-done = f32[64,2048]{1,0:T(8,128)} async-done(((f32[256,2048]{1,0:T(8,128)}), f32[64,2048]{1,0:T(8,128)}) %reduce-scatter.2.cloned.1.call-update) | async-done | bytes 524304 | tf_op jit(solution)/shard_map/reduce_scatter | solution.py:66
  112.5 1.8 %convert_element_type.23 = bf16[64,2048]{1,0:T(8,128)(2,1)} convert(f32[64,2048]{1,0:T(8,128)} %reduce-scatter.2.cloned.1.call-done) | non-fusion elementwise | flops 131072 | bytes 786432 | tf_op jit(solution)/shard_map/convert_element_type | solution.py:73
  (8 shorter events, 0.1 us)
Async XLA Ops:
  7.2 29.6 %copy-start = (bf16[64,2048]{1,0:T(8,128)(2,1)S(1)}, bf16[64,2048]{1,0:T(8,128)(2,1)}, u32[]{:S(2)}) copy-start(bf16[64,2048]{1,0:T(8,128)(2,1)} %param.5) | copy-start | bytes 786436
  7.2 42.2 %all-gather.2.cloned.1.call-start = ((), (), s32[]{:S(2)}) async-start(), calls=%async_computation.1 | async-start | bytes 1310720 | tf_op jit(solution)/shard_map/all_gather | solution.py:51
  7.2 11.6 %collective-permute-start = (bf16[64,2048]{1,0:T(8,128)(2,1)}, bf16[64,2048]{1,0:T(8,128)(2,1)S(1)}, u32[]{:S(2)}, u32[]{:S(2)}) collective-permute-start(bf16[64,2048]{1,0:T(8,128)(2,1)} %param.5), channel_id=1, source_target_pairs={{0,1},{1,2},{2,3},{3,0},{4,5},{5,6},{6,7},{7,4},{8,9},{9,10},{10,1... | collective-permute-start | bytes 786440 | tf_op jit(solution)/shard_map/ppermute | solution.py:19
  18.8 11.0 %collective-permute-start.1 = (bf16[64,2048]{1,0:T(8,128)(2,1)S(1)}, bf16[64,2048]{1,0:T(8,128)(2,1)S(1)}, u32[]{:S(2)}, u32[]{:S(2)}) collective-permute-start(bf16[64,2048]{1,0:T(8,128)(2,1)S(1)} %collective-permute-done), channel_id=1, source_target_pairs={{0,1},{1,2},{2,3},{3,0},{4,5},{5,6},{6,7},{7,4},{8,9},{9,10},{10,1... | collective-permute-start | bytes 786440 | tf_op jit(solution)/shard_map/ppermute | solution.py:19
  18.8 17.8 %collective-permute-start.2 = (bf16[64,2048]{1,0:T(8,128)(2,1)}, bf16[64,2048]{1,0:T(8,128)(2,1)S(1)}, u32[]{:S(2)}, u32[]{:S(2)}) collective-permute-start(bf16[64,2048]{1,0:T(8,128)(2,1)} %param.5), channel_id=1, source_target_pairs={{0,3},{1,0},{2,1},{3,2},{4,7},{5,4},{6,5},{7,6},{8,11},{9,8},{10,9... | collective-permute-start | bytes 786440 | tf_op jit(solution)/shard_map/ppermute | solution.py:22
  22.7 89.8 %reduce-scatter.2.cloned.1.call-start = ((), (), s32[]{:S(2)}) async-start(), calls=%async_computation.2 | async-start | bytes 2621440 | tf_op jit(solution)/shard_map/reduce_scatter | solution.py:66
  36.8 6.6 %slice-start = ((s8[7340032]{0:T(1024)(128)(4,1)}), s8[4194304]{0:T(1024)(128)(4,1)S(1)}, s32[]{:S(2)}) async-start(s8[7340032]{0:T(1024)(128)(4,1)} %bitcast.11), calls=%async_computation.3 | async-start | bytes 8388608
  36.8 6.6 %slice-start.1 = ((s8[7340032]{0:T(1024)(128)(4,1)}), s8[3145728]{0:T(1024)(128)(4,1)S(1)}, s32[]{:S(2)}) async-start(s8[7340032]{0:T(1024)(128)(4,1)} %bitcast.11), calls=%async_computation.4 | async-start | bytes 6291456
  56.5 5.9 %copy-start.3 = (bf16[256,1792]{1,0:T(8,128)(2,1)}, bf16[256,1792]{1,0:T(8,128)(2,1)S(1)}, u32[]{:S(2)}) copy-start(bf16[256,1792]{1,0:T(8,128)(2,1)S(1)} %get-tuple-element.5) | copy-start | bytes 2752516
  56.5 5.9 %copy-start.2 = (bf16[256,1792]{1,0:T(8,128)(2,1)}, bf16[256,1792]{1,0:T(8,128)(2,1)S(1)}, u32[]{:S(2)}) copy-start(bf16[256,1792]{1,0:T(8,128)(2,1)S(1)} %get-tuple-element.4) | copy-start | bytes 2752516
  68.9 6.5 %copy-start.4 = (bf16[256,1792]{1,0:T(8,128)(2,1)S(1)}, bf16[256,1792]{1,0:T(8,128)(2,1)}, u32[]{:S(2)}) copy-start(bf16[256,1792]{1,0:T(8,128)(2,1)} %copy-done.3) | copy-start | bytes 2752516
  75.4 5.4 %copy-start.1 = (bf16[256,2048]{1,0:T(8,128)(2,1)S(1)}, bf16[256,2048]{1,0:T(8,128)(2,1)}, u32[]{:S(2)}) copy-start(bf16[256,2048]{1,0:T(8,128)(2,1)} %all-gather.2.cloned.1.call-done) | copy-start | bytes 3145732
  75.4 5.4 %copy-start.5 = (f32[256,1792]{1,0:T(8,128)S(1)}, f32[256,1792]{1,0:T(8,128)}, u32[]{:S(2)}) copy-start(f32[256,1792]{1,0:T(8,128)} %convolution_multiply_fusion) | copy-start | bytes 5505028
  75.4 5.4 %copy-start.6 = (f32[256,1792]{1,0:T(8,128)S(1)}, f32[256,1792]{1,0:T(8,128)}, u32[]{:S(2)}) copy-start(f32[256,1792]{1,0:T(8,128)} %convolution_multiply_fusion.1) | copy-start | bytes 5505028
Sparse Core Ops, SparseCore 0:
  22.8 26.5 all-gather.1
  69.1 43.4 reduce-scatter.1
